TPU v7x, 32 devices: a whole 2x2x4 slice. The times are simulated.
32 devices in a mesh: groups: 2 (over x), chan: 8 (over z, y), seq: 2 (over core).
Axes of the slice: x: 2, y: 2, z: 4, core: 2. Of those that a mesh axis runs over, the one named last changes fastest.
Arguments:
- tokens: bfloat16 [2048, 8192], P(('groups', 'seq'), 'chan'), parts along dimension 0, may hold values from -42 to 42
- norm_gain: float32 [8192], replicated, may hold values from 0.1 to 1.9
- in_weight: bfloat16 [3, 8192, 8192], P(None, None, 'chan'), may hold values from -0.0625 to 0.0625
- short_weight: float32 [3, 7, 8192], P(None, None, 'chan'), may hold values from -2 to 2
- log_decay: float32 [16, 8192], P(None, 'chan'), may hold values from -0.034 to 0
- residue: float32 [16, 8192], P(None, 'chan'), may hold values from -0.15625 to 0.15625
- skip: float32 [8192], P('chan'), may hold values from 0.1 to 1.9
- out_weight: bfloat16 [8192, 8192], P('chan'), may hold values from -0.09375 to 0.09375
Outputs:
- mixed: bfloat16 [2048, 8192], P(('groups', 'seq'), 'chan'), parts along dimension 0
There are 2 independent parts, one for each index of `groups`. A program takes and returns all parts, laid end to end along the dimension named above; an argument that names none is the same for every part. Nothing has to cross between parts.
All inputs are finite; a program needn't handle non-finite values.
Results may differ from a plain program's by a relative error of at most 0.0067.
Values may be sent and summed in bfloat16 or wider, within the bound.
A program may use at most 448 MiB of HBM per device.

v0:
```python
import jax
import jax.numpy as jnp
from jax import lax
from jax.sharding import PartitionSpec as P

EPSILON = 1e-06


def from_behind(block, axis, distance):
    devices = range(lax.axis_size(axis))
    route = [(i - distance, i) for i in devices if i - distance in devices]
    return lax.ppermute(block, axis, route)


def prefix(part, axis, combine, identity):
    place = lax.axis_index(axis)
    gathered = jax.tree.map(lambda a: lax.all_gather(a, axis), part)
    state = jax.tree.map(lambda a, e: jnp.zeros_like(a) + jnp.asarray(e, a.dtype), part, identity)

    def one(step, state):
        return combine(
            state, jax.tree.map(lambda a: lax.dynamic_index_in_dim(a, step, 0, False), gathered)
        )

    return lax.fori_loop(0, place, one, state)


def scan_pair(earlier, later):
    return (earlier[0] * later[0], earlier[1] * later[0] + later[1])


def per_device(tokens, norm_gain, in_weight, short_weight, log_decay, residue, skip, out_weight):
    tok_count = tokens.shape[0]
    chan_width = tokens.shape[1]
    model_width = norm_gain.shape[0]
    tap_count = short_weight.shape[1]
    tok_float = tokens.astype(jnp.float32)
    squares = lax.psum(jnp.sum(tok_float * tok_float, axis=1), "chan")
    inv_rms = lax.rsqrt(squares / model_width + EPSILON)[:, None]
    scaled = (
        lax.all_gather(tokens, "chan", axis=1, tiled=True).astype(jnp.float32) * norm_gain[None, :]
    ).astype(jnp.bfloat16)
    projected = jnp.einsum("td,kdc->ktc", scaled, in_weight, preferred_element_type=jnp.float32)
    proj = (projected * inv_rms[None]).astype(jnp.bfloat16)
    rim_rows = proj[:, tok_count - (tap_count - 1) :, :]
    earlier_rows = from_behind(rim_rows, "seq", 1)
    extended = jnp.concatenate([earlier_rows, proj], axis=1).astype(jnp.float32)
    conv = jnp.zeros((3, tok_count, chan_width), jnp.float32)
    for tap in range(tap_count):
        conv = (
            conv
            + short_weight[:, tap][:, None, :]
            * extended[:, tap_count - 1 - tap : tap_count - 1 - tap + tok_count, :]
        )
    query = conv[0]
    product = conv[1] * conv[2]
    blk_size = min(128, tok_count)
    blk_count = tok_count // blk_size
    positions = jnp.arange(blk_size, dtype=jnp.float32)
    pole_power = jnp.exp(positions[:, None, None] * log_decay[None])
    weighted = pole_power * residue[None]
    filt_rows = jnp.sum(weighted, axis=1).T
    padded_filt = jnp.concatenate(
        [filt_rows[:, :1], jnp.zeros((chan_width, blk_size), jnp.float32), filt_rows[:, :0:-1]],
        axis=1,
    )
    tiled = jnp.tile(padded_filt, (1, blk_size))[:, : blk_size * (2 * blk_size - 1)]
    toeplitz = tiled.reshape(chan_width, blk_size, 2 * blk_size - 1)[:, :, :blk_size]
    product_blocks = product.reshape(blk_count, blk_size, chan_width)
    inner_part = jnp.einsum(
        "cts,ksc->ktc", toeplitz, product_blocks, precision=lax.Precision.HIGHEST
    )
    back_power = jnp.exp((blk_size - positions)[:, None, None] * log_decay[None])
    block_states = jnp.einsum(
        "ksc,snc->knc", product_blocks, back_power, precision=lax.Precision.HIGHEST
    )
    block_decay = jnp.exp(blk_size * log_decay)
    carried = jnp.zeros_like(log_decay)
    entering = []
    for span_idx in range(blk_count):
        entering.append(carried)
        carried = block_decay * carried + block_states[span_idx]
    shard_decay = jnp.exp(tok_count * log_decay)
    unused_decay, state_in = prefix(
        (shard_decay, carried),
        "seq",
        scan_pair,
        (jnp.ones_like(log_decay), jnp.zeros_like(log_decay)),
    )
    span_starts = jnp.arange(blk_count, dtype=jnp.float32) * blk_size
    lead_decay = jnp.exp(span_starts[:, None, None] * log_decay[None])
    entry_states = lead_decay * state_in[None] + jnp.stack(entering)
    carry_part = jnp.einsum("tnc,knc->ktc", weighted, entry_states, precision=lax.Precision.HIGHEST)
    long_conv = (inner_part + carry_part).reshape(tok_count, chan_width)
    gated = (query * (long_conv + skip[None, :] * product)).astype(jnp.bfloat16)
    partial_sums = jnp.dot(gated, out_weight, preferred_element_type=jnp.float32)
    branch_out = lax.psum_scatter(partial_sums, "chan", scatter_dimension=1, tiled=True)
    return (tok_float + branch_out).astype(jnp.bfloat16)


def solution(mesh):
    return jax.shard_map(
        per_device,
        mesh=mesh,
        in_specs=(
            P(("groups", "seq"), "chan"),
            P(),
            P(None, None, "chan"),
            P(None, None, "chan"),
            P(None, "chan"),
            P(None, "chan"),
            P("chan"),
            P("chan", None),
        ),
        out_specs=P(("groups", "seq"), "chan"),
        check_vma=False,
    )
```

profile of v0, /device:TPU:1, one launch (start us, length us, event | category | flops | bytes accessed | tf_op | source)
XLA Modules:
  0.0 1110.5 jit_solution(7528255123943374717)
XLA Ops:
  9.5 11.7 %fusion.9 = f32[128,1024]{0,1:T(8,128)S(1)} fusion(f32[16,1024]{0,1:T(8,128)S(1)} %copy.56, f32[16,1024]{0,1:T(8,128)S(1)} %copy.55), kind=kLoop, calls=%fused_computation.12 | loop fusion | flops 6160384 | bytes 655360 | tf_op jit(solution)/shard_map/reduce_sum | solution.py:62
  22.5 20.1 %psum.7 = f32[512]{0:T(512)S(1)} all-reduce(f32[512]{0:T(512)S(1)} %fusion.22), channel_id=1, replica_groups=mesh['groups'=2,'chan'=8,'seq'=2] {'chan'}, use_global_device_ids=true, to_apply=%region_1.0 | all-reduce | flops 512 | bytes 4096 | tf_op jit(solution)/shard_map/psum | solution.py:38
  45.2 90.5 %all-gather.4.cloned.1.call-done = bf16[512,8192]{1,0:T(8,128)(2,1)} async-done(((bf16[512,1024]{1,0:T(8,128)(2,1)}), bf16[512,8192]{1,0:T(8,128)(2,1)}) %all-gather.4.cloned.1.call-update) | async-done | bytes 8388624 | tf_op jit(solution)/shard_map/all_gather | solution.py:41
  135.7 33.8 %fusion.21 = bf16[3,512,1024]{2,1,0:T(8,128)(2,1)S(1)} fusion(f32[512]{0:T(512)S(1)} %add_rsqrt_fusion, bf16[3,8192,1024]{2,1,0:T(8,128)(2,1)} %param.12, bf16[512,8192]{1,0:T(8,128)(2,1)} %all-gather.4.cloned.1.call-done, f32[8192]{0:T(1024)S(1)} %copy-done.20), kind=kOutput, calls=%fused_computation.33 | convolution fusion | flops 25785532416 | bytes 61900800 | tf_op jit(solution)/shard_map/td,kdc->ktc/dot_general | solution.py:43
  172.8 41.1 %tile.4 = f32[1024,128,256]{2,1,0:T(8,128)} broadcast(f32[1024,256]{1,0:T(8,128)S(1)} %pad_maximum_fusion), dimensions={0,2} | broadcast | bytes 135266304 | tf_op jit(solution)/shard_map/tile | solution.py:67
  213.9 108.6 %copy.69 = f32[128,8,128,256]{3,1,2,0:T(8,128)} copy(f32[128,8,128,256]{3,2,1,0:T(8,128)} %bitcast.28) | data formatting | bytes 268435456
  322.5 87.6 %slice.117 = f32[1024,32640]{1,0:T(8,128)} slice(f32[1024,32768]{1,0:T(8,128)} %bitcast.29), slice={[0:1024], [0:32640]} | slice | bytes 267386880 | tf_op jit(solution)/shard_map/slice | solution.py:67
  410.0 211.3 %reshape.29 = f32[1024,128,255]{2,1,0:T(8,128)} reshape(f32[1024,32640]{1,0:T(8,128)} %slice.117) | data formatting | bytes 267386880 | tf_op jit(solution)/shard_map/reshape | solution.py:68
  621.4 4.4 maximum_convert_fusion
  625.8 19.9 %fusion.11 = f32[3,512,1024]{2,1,0:T(8,128)} fusion(f32[3,518,1024]{2,1,0:T(8,128)} %maximum_convert_fusion, f32[3,1024]{1,0:T(4,128)S(1)} %copy-done.11, f32[3,1024]{1,0:T(4,128)S(1)} %copy-done.12, f32[3,1024]{1,0:T(4,128)S(1)} %copy-done.13, f32[3,1024]{1,0:T(4,128)S(1)} %copy-done.14, f32[3,1024]{1,0:T(4,128)S(1)} %copy-done.15, ...), kind=kLoop, calls=%fused_computation.15 | loop fusion | flops 20447232 | bytes 50417664 | tf_op jit(solution)/shard_map/add | solution.py:51
  645.7 4.1 slice_multiply_fusion.7
  649.8 2.0 copy.57
  651.9 110.2 %fusion = f32[1024,4,128]{2,1,0:T(4,128)} fusion(f32[4,128,1024]{1,0,2:T(4,128)S(1)} %copy.57, f32[1024,128,255]{2,1,0:T(8,128)} %reshape.29), kind=kOutput, calls=%fused_computation.2 | convolution fusion | flops 805306368 | bytes 71303168 | tf_op jit(solution)/shard_map/cts,ksc->ktc/dot_general | solution.py:70
  762.1 14.8 %fusion.5 = f32[1024,16,4]{1,2,0:T(4,128)} fusion(f32[4,128,1024]{1,0,2:T(4,128)S(1)} %copy.57, f32[128]{0:T(128)S(1)} %copy-done.21, f32[16,1024]{0,1:T(8,128)S(1)} %copy-done.9), kind=kOutput, calls=%fused_computation.7 | convolution fusion | flops 102760448 | bytes 2425344 | tf_op jit(solution)/shard_map/ksc,snc->knc/dot_general | solution.py:74
  776.9 2.0 copy.59
  779.6 3.5 all-gather
  783.1 1.9 all-gather.1
  786.1 1.9 copy.60
  788.0 12.9 %add_bitcast_fusion = f32[4,128,1024]{1,0,2:T(4,128)} fusion(f32[1024,4,128]{2,1,0:T(4,128)S(1)} %copy-done.2, f32[4,16,1024]{1,0,2:T(4,128)} %copy.60, f32[16,1024]{0,1:T(8,128)S(1)} %copy-done.7, f32[16,1024]{0,1:T(8,128)S(1)} %copy-done.9), kind=kOutput, calls=%fused_computation.44 | convolution fusion | flops 105381888 | bytes 4587520 | tf_op jit(solution)/shard_map/tnc,knc->ktc/dot_general | solution.py:93
  800.9 1.9 copy.61
  802.8 3.7 fusion.25
  806.5 15.6 %fusion.37 = f32[512,8192]{1,0:T(8,128)} fusion(bf16[512,1024]{1,0:T(8,128)(2,1)S(1)} %fusion.25, bf16[1024,8192]{1,0:T(8,128)(2,1)} %param.17), kind=kOutput, calls=%fused_computation.71 | convolution fusion | flops 8589934592 | bytes 34603008 | tf_op jit(solution)/shard_map/dot_general | solution.py:96
  822.2 278.4 %reduce-scatter.2.cloned.1.call-done = f32[512,1024]{1,0:T(8,128)} async-done(((f32[512,8192]{1,0:T(8,128)}), f32[512,1024]{1,0:T(8,128)}) %reduce-scatter.2.cloned.1.call-update) | async-done | bytes 2097168 | tf_op jit(solution)/shard_map/reduce_scatter | solution.py:97
  1100.5 2.9 fusion.23
  (73 shorter events, 11.9 us)
Async XLA Ops:
  6.5 15.7 %copy-start = (bf16[512,1024]{1,0:T(8,128)(2,1)S(1)}, bf16[512,1024]{1,0:T(8,128)(2,1)}, u32[]{:S(2)}) copy-start(bf16[512,1024]{1,0:T(8,128)(2,1)} %param.10) | copy-start | bytes 3145732
  6.5 36.6 %copy-start.10 = (f32[3,7,1024]{2,1,0:T(8,128)S(1)}, f32[3,7,1024]{2,1,0:T(8,128)}, u32[]{:S(2)}) copy-start(f32[3,7,1024]{2,1,0:T(8,128)} %param.13) | copy-start | bytes 258052
  6.5 129.2 %copy-start.20 = (f32[8192]{0:T(1024)S(1)}, f32[8192]{0:T(1024)}, u32[]{:S(2)}) copy-start(f32[8192]{0:T(1024)} %param.11) | copy-start | bytes 98308
  6.5 129.2 %all-gather.4.cloned.1.call-start = ((), (), s32[]{:S(2)}) async-start(), calls=%async_computation.1 | async-start | bytes 9437184 | tf_op jit(solution)/shard_map/all_gather | solution.py:41
  7.3 1093.3 %reduce-scatter.2.cloned.1.call-start = ((), (), s32[]{:S(2)}) async-start(), calls=%async_computation.2 | async-start | bytes 18874368 | tf_op jit(solution)/shard_map/reduce_scatter | solution.py:97
  8.3 12.9 %copy-start.6 = (f32[16,1024]{0,1:T(8,128)}, f32[16,1024]{0,1:T(8,128)S(1)}, u32[]{:S(2)}) copy-start(f32[16,1024]{0,1:T(8,128)S(1)} %copy.56) | copy-start | bytes 196612
  9.4 11.8 %copy-start.8 = (f32[16,1024]{0,1:T(8,128)}, f32[16,1024]{0,1:T(8,128)S(1)}, u32[]{:S(2)}) copy-start(f32[16,1024]{0,1:T(8,128)S(1)} %copy.55) | copy-start | bytes 196612
  169.5 44.4 %copy-start.3 = (bf16[3,512,1024]{2,1,0:T(8,128)(2,1)}, bf16[3,512,1024]{2,1,0:T(8,128)(2,1)S(1)}, u32[]{:S(2)}) copy-start(bf16[3,512,1024]{2,1,0:T(8,128)(2,1)S(1)} %fusion.21) | copy-start | bytes 9437188
  170.2 451.1 %collective-permute-start = (bf16[3,6,1024]{2,1,0:T(8,128)(2,1)}, bf16[3,6,1024]{2,1,0:T(8,128)(2,1)}, u32[]{:S(2)}, u32[]{:S(2)}) collective-permute-start(bf16[3,6,1024]{2,1,0:T(8,128)(2,1)} %slice.104), channel_id=1, source_target_pairs={{0,1},{2,3},{4,5},{6,7},{8,9},{10,11},{12,13},{14,15},{16,17},{18,... | collective-permute-start | bytes 110600 | tf_op jit(solution)/shard_map/ppermute | solution.py:12
  410.0 211.3 %copy-start.4 = (bf16[3,512,1024]{2,1,0:T(8,128)(2,1)S(1)}, bf16[3,512,1024]{2,1,0:T(8,128)(2,1)}, u32[]{:S(2)}) copy-start(bf16[3,512,1024]{2,1,0:T(8,128)(2,1)} %copy-done.3) | copy-start | bytes 9437188
  621.3 4.5 copy-start.12
  621.3 4.5 copy-start.13
  621.3 4.5 copy-start.14
  621.3 4.5 copy-start.15
  621.3 4.5 copy-start.16
  621.3 4.5 copy-start.17
  651.9 110.2 %copy-start.9 = (f32[16,1024]{0,1:T(8,128)S(1)}, f32[16,1024]{0,1:T(8,128)}, u32[]{:S(2)}) copy-start(f32[16,1024]{0,1:T(8,128)} %copy-done.8) | copy-start | bytes 196612
  651.9 110.2 %copy-start.21 = (f32[128]{0:T(128)S(1)}, f32[128]{0:T(128)}, u32[]{:S(2)}) copy-start(f32[128]{0:T(128)} %iota_subtract_fusion) | copy-start | bytes 1540
  762.1 16.9 %copy-start.5 = (f32[16,1024]{1,0:T(8,128)S(1)}, f32[16,1024]{1,0:T(8,128)}, u32[]{:S(2)}) copy-start(f32[16,1024]{1,0:T(8,128)} %param.14) | copy-start | bytes 196612
  762.1 23.0 %copy-start.19 = (f32[4]{0:T(128)S(1)}, f32[4]{0:T(128)}, u32[]{:S(2)}) copy-start(f32[4]{0:T(128)} %iota_multiply_fusion) | copy-start | bytes 52
  762.1 25.9 %copy-start.7 = (f32[16,1024]{0,1:T(8,128)S(1)}, f32[16,1024]{0,1:T(8,128)}, u32[]{:S(2)}) copy-start(f32[16,1024]{0,1:T(8,128)} %copy-done.6) | copy-start | bytes 196612
  776.9 11.1 copy-start.2
  788.0 14.8 %copy-start.18 = (f32[1024]{0:T(1024)S(1)}, f32[1024]{0:T(1024)}, u32[]{:S(2)}) copy-start(f32[1024]{0:T(1024)} %param.16) | copy-start | bytes 12292
  822.1 278.4 %copy-start.1 = (bf16[512,1024]{1,0:T(8,128)(2,1)S(1)}, bf16[512,1024]{1,0:T(8,128)(2,1)}, u32[]{:S(2)}) copy-start(bf16[512,1024]{1,0:T(8,128)(2,1)} %param.10) | copy-start | bytes 3145732
  (1 other events, 4.5 us)
Sparse Core Ops, SparseCore 0:
  9.5 126.1 all-gather.3
  822.3 278.1 reduce-scatter.1
where the time goes:
time: 1120 us; the launch traced here: 1110 us
  local copies, waits for them, and re-layouts  463 us (41%)
  waiting for transfers between devices  370 us (33%)
  matrix products  187 us (17%)
  other arithmetic  50 us (4%)
  blocking collectives  25.5 us (2%)
  between operations  13.9 us (1%)
    reduce_scatter x1, waiting for transfers between devices, per_device(): lax.psum_scatter(partial_sums, 'chan', scatter_dimension=1, tiled=True)  278 us
    reshape x1, local copies, waits for them, and re-layouts, per_device(): tiled.reshape(chan_width, blk_size, 2 * blk_size - 1)[:, :, :blk_size]  211 us
    unnamed x51, local copies, waits for them, and re-layouts  113 us
    dot_general x1, matrix products, per_device(): jnp.einsum('cts,ksc->ktc', toeplitz, product_blocks, precision=lax.Precis...  110 us
    all_gather x1, waiting for transfers between devices, per_device(): lax.all_gather(tokens, 'chan', axis=1, tiled=True).astype(jnp.float32)  90.5 us
    slice x1, local copies, waits for them, and re-layouts, per_device(): jnp.tile(padded_filt, (1, blk_size))[:, :blk_size * (2 * blk_size - 1)]  87.6 us
    another operation x1, local copies, waits for them, and re-layouts, per_device(): jnp.tile(padded_filt, (1, blk_size))[:, :blk_size * (2 * blk_size - 1)]  41.1 us
    dot_general x1, matrix products, per_device(): jnp.einsum('td,kdc->ktc', scaled, in_weight, preferred_element_type=jnp.f...  33.8 us
  transfers between devices with their start and end apart: 3, of which 2 were waited for; matrix products, arithmetic and copies ran while one was open for 42% of the time, Pallas kernels for 0%

commit v1 on v0

v1 whole, which is shorter than its diff:
```python
import functools

import jax
import jax.numpy as jnp
from jax import lax
from jax.experimental import pallas as pl
from jax.experimental.pallas import tpu as pltpu
from jax.sharding import PartitionSpec as P

EPSILON = 1e-06
MESH = pl.DeviceIdType.MESH
PIECES = 2
W_SLOTS = 4


def ring_position(index, n):
    odd = lax.rem(index, 2)
    return (1 - odd) * lax.div(index, 2) + odd * (n - 1 - lax.div(index, 2))


def ring_index(position, n):
    back = lax.div(position, n // 2)
    return (1 - back) * (2 * position) + back * (2 * (n - 1 - position) + 1)


def greet(peers):
    barrier = pltpu.get_barrier_semaphore()
    for peer in peers:
        pl.semaphore_signal(barrier, inc=1, device_id=peer, device_id_type=MESH)
    pl.semaphore_wait(barrier, len(peers))


def strided(start, size, stride):
    return pl.ds(start, size) if stride == 1 else pl.ds(start, size, stride=stride)


def front_kernel(
    n, eps, tok_hbm, gain_ref, w_hbm, taps_ref, decay_ref, res_ref, skip_ref, gated_ref,
    held, acc, w_buf, scaled, squares, query, signal_rows, pole, residue, skip_rows,
    rim_out, rim_in, state_out, state_in, send_sem, recv_sem, w_sem, own_sem, pair_send, pair_recv,
):
    rows, width = tok_hbm.shape
    half = rows // 2
    piece = half // PIECES
    groups = width // 128
    poles = decay_ref.shape[0]
    tap_count = taps_ref.shape[1]
    chunk = min(64, half)
    tile = min(256, width)
    me = lax.axis_index("chan")
    seq = lax.axis_index("seq")
    pos = ring_position(me, n)
    right = {"chan": ring_index(lax.rem(pos + 1, n), n)}
    left = {"chan": ring_index(lax.rem(pos + n - 1, n), n)}
    partner = {"seq": 1 - seq}
    ahead = (right, left)

    def owner_of(direction, step):
        shift = lax.rem(pos + n - step, n) if direction == 0 else lax.rem(pos + step, n)
        return ring_index(shift, n)

    def owner_dyn(direction, step):
        return ring_index(lax.rem(pos + (1 - direction) * (n - step) + direction * step, n), n)

    def w_copy(g):
        unit = lax.div(g, 3)
        owner = owner_dyn(lax.rem(unit, 2), lax.div(unit, 2))
        slot = lax.rem(g, W_SLOTS)
        return pltpu.make_async_copy(
            w_hbm.at[lax.rem(g, 3), pl.ds(pl.multiple_of(owner * width, 128), width), :],
            w_buf.at[slot],
            w_sem.at[slot],
        )

    def hop(direction, step, part, block_step):
        owner = owner_of(direction, block_step)
        span = pl.ds(direction * half + part * piece, piece)
        return pltpu.make_async_remote_copy(
            src_ref=held.at[owner, span, :],
            dst_ref=held.at[owner, span, :],
            send_sem=send_sem.at[direction, step, part],
            recv_sem=recv_sem.at[direction, step, part],
            device_id=ahead[direction],
            device_id_type=MESH,
        )

    own = pltpu.make_async_copy(tok_hbm, held.at[me], own_sem)
    own.start()
    for g in range(W_SLOTS):
        w_copy(jnp.int32(g)).start()
    greet((right, left, partner))
    own.wait()
    for part in range(PIECES):
        for direction in range(2):
            hop(direction, 0, part, 0).start()

    @pl.loop(0, rows // chunk)
    def _(b):
        r = pl.multiple_of(b * chunk, chunk)
        squares[pl.ds(r, chunk), :] = jnp.zeros((chunk, 128), jnp.float32)
        for i in range(3):
            acc[i, pl.ds(r + 8, chunk), :] = jnp.zeros((chunk, width), jnp.float32)

    for j in range(groups):
        lanes = pl.ds(j * 128, 128)
        pole[strided(j, poles, groups), :] = jnp.exp(decay_ref[:, lanes])
        residue[strided(j, poles, groups), :] = res_ref[:, lanes]
        skip_rows[pl.ds(j, 1), :] = skip_ref[:, lanes]

    def compute(step, direction):
        owner = owner_of(direction, step)
        first = direction * half
        gain = gain_ref[:, pl.ds(pl.multiple_of(owner * width, 128), width)]
        small = min(32, half)

        @pl.loop(0, half // small)
        def _(b):
            r = pl.multiple_of(b * small, small)
            x = held[owner, pl.ds(first + r, small), :].astype(jnp.float32)
            scaled[pl.ds(r, small), :] = (x * gain).astype(jnp.bfloat16)
            total = squares[pl.ds(first + r, small), :]
            for j in range(groups):
                xj = x[:, j * 128 : (j + 1) * 128]
                total = total + xj * xj
            squares[pl.ds(first + r, small), :] = total

        @pl.loop(0, 3)
        def _(i):
            g = (step * 2 + direction) * 3 + i
            slot = lax.rem(g, W_SLOTS)
            w_copy(g).wait()

            @pl.loop(0, width // tile)
            def _(c):
                cols = pl.ds(pl.multiple_of(c * tile, 128), tile)
                acc[i, pl.ds(first + 8, half), cols] += jnp.dot(
                    scaled[...], w_buf[slot, :, cols], preferred_element_type=jnp.float32
                )

            @pl.when(g + W_SLOTS < n * 6)
            def _():
                w_copy(g + W_SLOTS).start()

    @pl.loop(1, n)
    def _(step):
        for part in range(PIECES):
            for direction in range(2):
                hop(direction, step - 1, part, step).wait_recv()

                @pl.when(step < n - 1)
                def _():
                    hop(direction, step, part, step).start()

            compute(step - 1, part)

    @pl.loop(n - 1, n)
    def _(step):
        for direction in range(2):
            compute(step, direction)

    @pl.loop(0, rows // chunk)
    def _(b):
        r = pl.multiple_of(b * chunk, chunk)
        mean = jnp.sum(squares[pl.ds(r, chunk), :], axis=1, keepdims=True) / (n * width)
        inv = lax.rsqrt(mean + eps)
        for i in range(3):
            span = pl.ds(r + 8, chunk)
            acc[i, span, :] = (acc[i, span, :] * inv).astype(jnp.bfloat16).astype(jnp.float32)

    rim_out[...] = acc[:, pl.ds(rows, 8), :]
    rim = pltpu.make_async_remote_copy(
        src_ref=rim_out, dst_ref=rim_in, send_sem=pair_send.at[0], recv_sem=pair_recv.at[0],
        device_id=partner, device_id_type=MESH,
    )
    rim.start()
    rim.wait()
    acc[:, pl.ds(0, 8), :] = jnp.where(seq > 0, rim_in[...], 0.0)

    @pl.loop(0, groups)
    def _(j):
        lanes = pl.ds(pl.multiple_of(j * 128, 128), 128)

        @pl.loop(0, rows // chunk)
        def _(b):
            r = pl.multiple_of(b * chunk, chunk)
            conv = []
            for i in range(3):
                x = acc[i, pl.ds(r, chunk + 8), lanes]
                total = x[8:, :] * taps_ref[i, pl.ds(0, 1), lanes]
                for tap in range(1, tap_count):
                    shifted = pltpu.roll(x, tap, 0)[8:, :]
                    total = total + shifted * taps_ref[i, pl.ds(tap, 1), lanes]
                conv.append(total)
            query[pl.ds(r, chunk), lanes] = conv[0]
            signal_rows[strided(r * groups + j, chunk, groups), :] = conv[1] * conv[2]

    def row_at(t):
        return pl.ds(pl.multiple_of(t * groups, groups), groups)

    poles_held = [pole[pl.ds(k * groups, groups), :] for k in range(poles)]

    def only_state(t, state):
        row = signal_rows[row_at(t), :]
        return tuple(poles_held[k] * state[k] + row for k in range(poles))

    zero = tuple(jnp.zeros((groups, 128), jnp.float32) for _ in range(poles))
    last = lax.fori_loop(0, rows, only_state, zero, unroll=8)
    for k in range(poles):
        state_out[pl.ds(k * groups, groups), :] = last[k]
    carry = pltpu.make_async_remote_copy(
        src_ref=state_out, dst_ref=state_in, send_sem=pair_send.at[1], recv_sem=pair_recv.at[1],
        device_id=partner, device_id_type=MESH,
    )
    carry.start()
    carry.wait()
    res_held = [residue[pl.ds(k * groups, groups), :] for k in range(poles)]
    skip_held = skip_rows[...]

    def with_output(t, state):
        row = signal_rows[row_at(t), :]
        state = tuple(poles_held[k] * state[k] + row for k in range(poles))
        terms = [res_held[k] * state[k] for k in range(poles)]
        while len(terms) > 1:
            terms = [a + b for a, b in zip(terms[::2], terms[1::2])] + terms[len(terms) // 2 * 2 :]
        signal_rows[row_at(t), :] = terms[0] + skip_held * row
        return state

    entry = tuple(
        jnp.where(seq > 0, state_in[pl.ds(k * groups, groups), :], 0.0) for k in range(poles)
    )
    lax.fori_loop(0, rows, with_output, entry, unroll=4)

    @pl.loop(0, groups)
    def _(j):
        lanes = pl.ds(pl.multiple_of(j * 128, 128), 128)

        @pl.loop(0, rows // chunk)
        def _(b):
            r = pl.multiple_of(b * chunk, chunk)
            long = signal_rows[strided(r * groups + j, chunk, groups), :]
            gated_ref[pl.ds(r, chunk), lanes] = (query[pl.ds(r, chunk), lanes] * long).astype(jnp.bfloat16)

    @pl.loop(0, n - 1)
    def _(step):
        for part in range(PIECES):
            for direction in range(2):
                hop(direction, step, part, step).wait_send()


def back_kernel(
    n, gated_ref, tok_ref, w_hbm, out_ref, w_buf, partial, outgoing, incoming, send_sem, recv_sem, w_sem
):
    rows, width = tok_ref.shape
    half = rows // 2
    piece = half // PIECES
    tile = min(256, width)
    me = lax.axis_index("chan")
    pos = ring_position(me, n)
    right = {"chan": ring_index(lax.rem(pos + 1, n), n)}
    left = {"chan": ring_index(lax.rem(pos + n - 1, n), n)}
    ahead = (right, left)

    def w_copy(direction, step):
        if direction == 0:
            target = ring_index(lax.rem(pos + 2 * n - 1 - step, n), n)
        else:
            target = ring_index(lax.rem(pos + 1 + step, n), n)
        slot = lax.rem(step, 2)
        return pltpu.make_async_copy(
            w_hbm.at[:, pl.ds(pl.multiple_of(target * width, 128), width)],
            w_buf.at[direction, slot],
            w_sem.at[direction, slot],
        )

    def hop(direction, step, part):
        span = pl.ds(part * piece, piece)
        return pltpu.make_async_remote_copy(
            src_ref=outgoing.at[direction, step, span, :],
            dst_ref=incoming.at[direction, step, span, :],
            send_sem=send_sem.at[direction, step, part],
            recv_sem=recv_sem.at[direction, step, part],
            device_id=ahead[direction],
            device_id_type=MESH,
        )

    def multiply(step):
        for direction in range(2):
            w_copy(direction, step).wait()
            slot = lax.rem(step, 2)

            @pl.loop(0, width // tile)
            def _(c):
                cols = pl.ds(pl.multiple_of(c * tile, 128), tile)
                partial[direction, :, cols] = jnp.dot(
                    gated_ref[pl.ds(direction * half, half), :],
                    w_buf[direction, slot, :, cols],
                    preferred_element_type=jnp.float32,
                )

            @pl.when(step + 2 < n)
            def _():
                w_copy(direction, step + 2).start()

    for step in range(2):
        for direction in range(2):
            w_copy(direction, jnp.int32(step)).start()
    greet((right, left))
    small = min(32, piece)
    multiply(jnp.int32(0))
    for part in range(PIECES):
        for direction in range(2):

            @pl.loop(0, piece // small)
            def _(b):
                r = pl.multiple_of(part * piece + b * small, small)
                outgoing[direction, 0, pl.ds(r, small), :] = partial[
                    direction, pl.ds(r, small), :
                ].astype(jnp.bfloat16)

            hop(direction, 0, part).start()

    @pl.loop(1, n - 1)
    def _(step):
        multiply(step)
        for part in range(PIECES):
            for direction in range(2):
                hop(direction, step - 1, part).wait_recv()

                @pl.loop(0, piece // small)
                def _(b):
                    r = pl.multiple_of(part * piece + b * small, small)
                    span = pl.ds(r, small)
                    outgoing[direction, step, span, :] = (
                        partial[direction, span, :]
                        + incoming[direction, step - 1, span, :].astype(jnp.float32)
                    ).astype(jnp.bfloat16)

                hop(direction, step, part).start()

    multiply(jnp.int32(n - 1))
    for part in range(PIECES):
        for direction in range(2):
            hop(direction, n - 2, part).wait_recv()

            @pl.loop(0, piece // small)
            def _(b):
                r = pl.multiple_of(part * piece + b * small, small)
                span = pl.ds(r, small)
                whole = pl.ds(direction * half + r, small)
                out_ref[whole, :] = (
                    tok_ref[whole, :].astype(jnp.float32)
                    + (
                        partial[direction, span, :]
                        + incoming[direction, n - 2, span, :].astype(jnp.float32)
                    )
                ).astype(jnp.bfloat16)

    @pl.loop(0, n - 1)
    def _(step):
        for part in range(PIECES):
            for direction in range(2):
                hop(direction, step, part).wait_send()


def per_device(n, tokens, norm_gain, in_weight, short_weight, log_decay, residue, skip, out_weight):
    rows, width = tokens.shape
    groups = width // 128
    poles = log_decay.shape[0]
    half = rows // 2
    vmem = pl.BlockSpec(memory_space=pltpu.VMEM)
    anywhere = pl.BlockSpec(memory_space=pl.ANY)
    f32, bf16 = jnp.float32, jnp.bfloat16
    dma = pltpu.SemaphoreType.DMA
    gated = pl.pallas_call(
        functools.partial(front_kernel, n, EPSILON),
        out_shape=jax.ShapeDtypeStruct((rows, width), bf16),
        in_specs=[anywhere, vmem, anywhere, vmem, vmem, vmem, vmem],
        out_specs=vmem,
        scratch_shapes=[
            pltpu.VMEM((n, rows, width), bf16),
            pltpu.VMEM((3, rows + 8, width), f32),
            pltpu.VMEM((W_SLOTS, width, width), bf16),
            pltpu.VMEM((half, width), bf16),
            pltpu.VMEM((rows, 128), f32),
            pltpu.VMEM((rows, width), f32),
            pltpu.VMEM((rows * groups, 128), f32),
            pltpu.VMEM((poles * groups, 128), f32),
            pltpu.VMEM((poles * groups, 128), f32),
            pltpu.VMEM((groups, 128), f32),
            pltpu.VMEM((3, 8, width), f32),
            pltpu.VMEM((3, 8, width), f32),
            pltpu.VMEM((poles * groups, 128), f32),
            pltpu.VMEM((poles * groups, 128), f32),
            dma((2, n - 1, PIECES)),
            dma((2, n - 1, PIECES)),
            dma((W_SLOTS,)),
            dma,
            dma((2,)),
            dma((2,)),
        ],
        compiler_params=pltpu.CompilerParams(
            collective_id=0, has_side_effects=True, vmem_limit_bytes=56 << 20
        ),
    )(tokens, norm_gain[None, :], in_weight, short_weight, log_decay, residue, skip[None, :])
    return pl.pallas_call(
        functools.partial(back_kernel, n),
        out_shape=jax.ShapeDtypeStruct((rows, width), bf16),
        in_specs=[vmem, vmem, anywhere],
        out_specs=vmem,
        scratch_shapes=[
            pltpu.VMEM((2, 2, width, width), bf16),
            pltpu.VMEM((2, half, width), f32),
            pltpu.VMEM((2, n - 1, half, width), bf16),
            pltpu.VMEM((2, n - 1, half, width), bf16),
            dma((2, n - 1, PIECES)),
            dma((2, n - 1, PIECES)),
            dma((2, 2)),
        ],
        compiler_params=pltpu.CompilerParams(
            collective_id=1, has_side_effects=True, vmem_limit_bytes=56 << 20
        ),
    )(gated, tokens, out_weight)


def solution(mesh):
    return jax.shard_map(
        functools.partial(per_device, mesh.shape["chan"]),
        mesh=mesh,
        in_specs=(
            P(("groups", "seq"), "chan"),
            P(),
            P(None, None, "chan"),
            P(None, None, "chan"),
            P(None, "chan"),
            P(None, "chan"),
            P("chan"),
            P("chan", None),
        ),
        out_specs=P(("groups", "seq"), "chan"),
        check_vma=False,
    )
```

time: 1120 us -> 208 us (0.19)
  local copies, waits for them, and re-layouts: 463 us -> 2.26 us
  waiting for transfers between devices: 370 us -> 0 us
  Pallas kernels: 0 us -> 204 us
  matrix products: 187 us -> 0 us
  other arithmetic: 50 us -> 0 us
  blocking collectives: 25.5 us -> 0 us
  between operations: 13.9 us -> 0.02 us
    reduce_scatter x1 -> x0, waiting for transfers between devices: 278 us -> none  [per_device(): lax.psum_scatter(partial_sums, 'chan', scatter_dimension=1, tiled=True)]
    reshape x1 -> x0, local copies, waits for them, and re-layouts: 211 us -> none  [per_device(): tiled.reshape(chan_width, blk_size, 2 * blk_size - 1)[:, :, :blk_size]]
    pallas_call x0 -> x2, Pallas kernels: none -> 204 us  [the longest x1 116 us: per_device(): pl.pallas_call(functools.partial(front_kernel, n, EPSILON), out_shape=jax...]
    dot_general x5 -> x0, matrix products: 187 us -> none  [the longest x1 110 us: per_device(): jnp.einsum('cts,ksc->ktc', toeplitz, product_blocks, precision=lax.Precis...]
    unnamed x51 -> x1, local copies, waits for them, and re-layouts: 113 us -> 2.26 us
    all_gather x1 -> x0, waiting for transfers between devices: 90.5 us -> none  [per_device(): lax.all_gather(tokens, 'chan', axis=1, tiled=True).astype(jnp.float32)]
    slice x4 -> x0, local copies, waits for them, and re-layouts: 88.5 us -> none  [the longest x1 87.6 us: per_device(): jnp.tile(padded_filt, (1, blk_size))[:, :blk_size * (2 * blk_size - 1)]]
    another operation x3 -> x0, local copies, waits for them, and re-layouts: 41.1 us -> none  [the longest x1 41.1 us: per_device(): jnp.tile(padded_filt, (1, blk_size))[:, :blk_size * (2 * blk_size - 1)]]
  transfers between devices with their start and end apart: 3 -> 0, of which waited for: 2 -> 0; matrix products, arithmetic and copies ran while one was open for 42% -> 0% of each run, Pallas kernels for 0% -> 0%
where the time goes in v1:
time: 208 us; the launch traced here: 207 us
  Pallas kernels  204 us (98%)
  local copies, waits for them, and re-layouts  2.26 us (1%)
    pallas_call x1, Pallas kernels, per_device(): pl.pallas_call(functools.partial(front_kernel, n, EPSILON), out_shape=jax...  116 us
    pallas_call x1, Pallas kernels, per_device(): pl.pallas_call(functools.partial(back_kernel, n), out_shape=jax.ShapeDtyp...  88.2 us

profile of v1, /device:TPU:1, one launch (start us, length us, event | category | flops | bytes accessed | tf_op | source)
XLA Modules:
  0.0 206.5 jit_solution(8077800774747975338)
XLA Ops:
  0.0 116.1 %shard_map.82.gated_ref = bf16[512,1024]{1,0:T(8,128)(2,1)} custom-call(bf16[512,1024]{1,0:T(8,128)(2,1)} %tok_ref.1, f32[1,8192]{1,0:T(1,128)} %bitcast.2, bf16[3,8192,1024]{2,1,0:T(8,128)(2,1)} %w_hbm.2, f32[3,7,1024]{2,1,0:T(8,128)} %taps_ref.1, f32[16,1024]{1,0:T(8,128)} %decay_ref.1, f32[16,1024]{1,0:T(8,128)} %res_ref.1, f32[1,1024]{1,0:T(1,128)} %bitcast.3), custom_call_target="tpu_custom_call" | custom-call | tf_op jit(solution)/shard_map/pallas_call | solution.py:374
  116.1 88.2 %shard_map.83 = bf16[512,1024]{1,0:T(8,128)(2,1)} custom-call(bf16[512,1024]{1,0:T(8,128)(2,1)} %shard_map.82.gated_ref, bf16[512,1024]{1,0:T(8,128)(2,1)} %tok_ref.1, bf16[1024,8192]{1,0:T(8,128)(2,1)} %w_hbm.3), custom_call_target="tpu_custom_call" | custom-call | tf_op jit(solution)/shard_map/pallas_call | solution.py:405
  204.3 2.3 %copy.10 = bf16[512,1024]{1,0:T(8,128)(2,1)} copy(bf16[512,1024]{1,0:T(8,128)(2,1)} %shard_map.83) | data formatting | bytes 2097152

commit v2 on v1

v2 whole, which is shorter than its diff:
```python
import functools

import jax
import jax.numpy as jnp
from jax import lax
from jax.experimental import pallas as pl
from jax.experimental.pallas import tpu as pltpu
from jax.sharding import PartitionSpec as P

EPSILON = 1e-06
MESH = pl.DeviceIdType.MESH
PIECES = 4
W_SLOTS = 4


def ring_position(index, n):
    odd = lax.rem(index, 2)
    return (1 - odd) * lax.div(index, 2) + odd * (n - 1 - lax.div(index, 2))


def ring_index(position, n):
    back = lax.div(position, n // 2)
    return (1 - back) * (2 * position) + back * (2 * (n - 1 - position) + 1)


def greet(peers):
    barrier = pltpu.get_barrier_semaphore()
    for peer in peers:
        pl.semaphore_signal(barrier, inc=1, device_id=peer, device_id_type=MESH)
    pl.semaphore_wait(barrier, len(peers))


def strided(start, size, stride):
    return pl.ds(start, size) if stride == 1 else pl.ds(start, size, stride=stride)


def front_kernel(
    n, eps, tok_hbm, gain_ref, w_hbm, taps_ref, decay_ref, res_ref, skip_ref, gated_ref,
    held, acc, w_buf, scaled, squares, query, signal_rows, pole, residue, skip_rows,
    rim_out, rim_in, state_out, state_in, first_state, send_sem, recv_sem, w_sem, own_sem, pair_send, pair_recv, turn,
):
    rows, width = tok_hbm.shape
    middle = n // 2
    piece = rows // PIECES
    groups = width // 128
    poles = decay_ref.shape[0]
    tap_count = taps_ref.shape[1]
    chunk = min(64, rows)
    tile = min(256, width)
    me = lax.axis_index("chan")
    seq = lax.axis_index("seq")
    pos = ring_position(me, n)
    right = {"chan": ring_index(lax.rem(pos + 1, n), n)}
    left = {"chan": ring_index(lax.rem(pos + n - 1, n), n)}
    partner = {"seq": 1 - seq}
    ahead = (right, left)

    def owner_of(block):
        away = lax.div(block + 1, 2)
        odd = lax.rem(block, 2)
        return ring_index(lax.rem(pos + odd * (n - away) + (1 - odd) * away, n), n)

    def w_copy(g):
        owner = owner_of(lax.div(g, 3))
        slot = lax.rem(g, W_SLOTS)
        return pltpu.make_async_copy(
            w_hbm.at[lax.rem(g, 3), pl.ds(pl.multiple_of(owner * width, 128), width), :],
            w_buf.at[slot],
            w_sem.at[slot],
        )

    def hop(direction, step, part, away):
        shift = pos + n - away if direction == 0 else pos + away
        owner = ring_index(lax.rem(shift, n), n)
        span = pl.ds(part * piece, piece)
        return pltpu.make_async_remote_copy(
            src_ref=held.at[owner, span, :],
            dst_ref=held.at[owner, span, :],
            send_sem=send_sem.at[direction, step, part],
            recv_sem=recv_sem.at[direction, step, part],
            device_id=ahead[direction],
            device_id_type=MESH,
        )

    own = pltpu.make_async_copy(tok_hbm, held.at[me], own_sem)
    own.start()
    for g in range(W_SLOTS):
        w_copy(jnp.int32(g)).start()
    greet((right, left, partner))
    own.wait()

    @pl.when(seq > 0)
    def _():
        pl.semaphore_wait(turn, 1)

    for part in range(PIECES):
        for direction in range(2):
            hop(direction, 0, part, 0).start()

    @pl.loop(0, rows // chunk)
    def _(b):
        r = pl.multiple_of(b * chunk, chunk)
        squares[pl.ds(r, chunk), :] = jnp.zeros((chunk, 128), jnp.float32)
        for i in range(3):
            acc[i, pl.ds(r + 8, chunk), :] = jnp.zeros((chunk, width), jnp.float32)

    for j in range(groups):
        lanes = pl.ds(j * 128, 128)
        pole[strided(j, poles, groups), :] = jnp.exp(decay_ref[:, lanes])
        residue[strided(j, poles, groups), :] = res_ref[:, lanes]
        skip_rows[pl.ds(j, 1), :] = skip_ref[:, lanes]

    def prepare(block):
        owner = owner_of(block)
        gain = gain_ref[:, pl.ds(pl.multiple_of(owner * width, 128), width)]
        small = min(32, rows)

        @pl.loop(0, rows // small)
        def _(b):
            r = pl.multiple_of(b * small, small)
            x = held[owner, pl.ds(r, small), :].astype(jnp.float32)
            scaled[pl.ds(r, small), :] = (x * gain).astype(jnp.bfloat16)
            total = squares[pl.ds(r, small), :]
            for j in range(groups):
                xj = x[:, j * 128 : (j + 1) * 128]
                total = total + xj * xj
            squares[pl.ds(r, small), :] = total

    def multiply(block, i):
        g = block * 3 + i
        slot = lax.rem(g, W_SLOTS)
        w_copy(g).wait()

        @pl.loop(0, width // tile)
        def _(c):
            cols = pl.ds(pl.multiple_of(c * tile, 128), tile)
            acc[i, pl.ds(8, rows), cols] += jnp.dot(
                scaled[...], w_buf[slot, :, cols], preferred_element_type=jnp.float32
            )

        @pl.when(g + W_SLOTS < n * 3)
        def _():
            w_copy(g + W_SLOTS).start()

    def arrive(step, part):
        for direction in range(2):
            hop(direction, step - 1, part, step).wait_recv()
            if part // (PIECES // 2) == direction:
                hop(direction, step, part, step).start()
            else:

                @pl.when(step < middle - 1)
                def _():
                    hop(direction, step, part, step).start()

    def pair_part(step, quarter):
        near = 2 * step - 1
        if quarter == 0:
            prepare(near)
            multiply(near, 0)
            multiply(near, 1)
        elif quarter == 1:
            multiply(near, 2)
        elif quarter == 2:
            prepare(near + 1)
            multiply(near + 1, 0)
            multiply(near + 1, 1)
        else:
            multiply(near + 1, 2)

    for part in range(PIECES):
        arrive(jnp.int32(1), part)
        if part == 0:
            prepare(jnp.int32(0))
        if part < 3:
            multiply(jnp.int32(0), part)

    @pl.loop(2, middle)
    def _(step):
        for part in range(PIECES):
            arrive(step, part)
            pair_part(step - 1, part)

    @pl.when(seq == 0)
    def _():
        pl.semaphore_signal(turn, inc=1, device_id=partner, device_id_type=MESH)

    for part in range(PIECES):
        pair_part(jnp.int32(middle - 1), part)
    for part in range(PIECES):
        hop(part // (PIECES // 2), middle - 1, part, middle).wait_recv()
    prepare(jnp.int32(n - 1))
    for i in range(3):
        multiply(jnp.int32(n - 1), i)

    @pl.loop(0, rows // chunk)
    def _(b):
        r = pl.multiple_of(b * chunk, chunk)
        mean = jnp.sum(squares[pl.ds(r, chunk), :], axis=1, keepdims=True) / (n * width)
        inv = lax.rsqrt(mean + eps)
        for i in range(3):
            span = pl.ds(r + 8, chunk)
            acc[i, span, :] = (acc[i, span, :] * inv).astype(jnp.bfloat16).astype(jnp.float32)

    rim_out[...] = acc[:, pl.ds(rows, 8), :]
    rim = pltpu.make_async_remote_copy(
        src_ref=rim_out, dst_ref=rim_in, send_sem=pair_send.at[0], recv_sem=pair_recv.at[0],
        device_id=partner, device_id_type=MESH,
    )

    @pl.when(seq == 0)
    def _():
        rim.start()

    @pl.when(seq > 0)
    def _():
        rim.wait_recv()

    acc[:, pl.ds(0, 8), :] = jnp.zeros((3, 8, width), jnp.float32)

    @pl.when(seq > 0)
    def _():
        acc[:, pl.ds(0, 8), :] = rim_in[...]


    @pl.loop(0, groups)
    def _(j):
        lanes = pl.ds(pl.multiple_of(j * 128, 128), 128)

        @pl.loop(0, rows // chunk)
        def _(b):
            r = pl.multiple_of(b * chunk, chunk)
            conv = []
            for i in range(3):
                x = acc[i, pl.ds(r, chunk + 8), lanes]
                total = x[8:, :] * taps_ref[i, pl.ds(0, 1), lanes]
                for tap in range(1, tap_count):
                    shifted = pltpu.roll(x, tap, 0)[8:, :]
                    total = total + shifted * taps_ref[i, pl.ds(tap, 1), lanes]
                conv.append(total)
            query[pl.ds(r, chunk), lanes] = conv[0]
            signal_rows[strided(r * groups + j, chunk, groups), :] = conv[1] * conv[2]

    def row_at(t):
        return pl.ds(pl.multiple_of(t * groups, groups), groups)

    poles_held = [pole[pl.ds(k * groups, groups), :] for k in range(poles)]

    carry = pltpu.make_async_remote_copy(
        src_ref=state_out, dst_ref=state_in, send_sem=pair_send.at[1], recv_sem=pair_recv.at[1],
        device_id=partner, device_id_type=MESH,
    )
    entry_rows = poles * groups

    @pl.when(seq == 0)
    def _():
        first_state[...] = jnp.zeros((entry_rows, 128), jnp.float32)

    @pl.when(seq > 0)
    def _():
        carry.wait_recv()
        first_state[...] = state_in[...]

    res_held = [residue[pl.ds(k * groups, groups), :] for k in range(poles)]
    skip_held = skip_rows[...]

    def with_output(t, state):
        row = signal_rows[row_at(t), :]
        state = tuple(poles_held[k] * state[k] + row for k in range(poles))
        terms = [res_held[k] * state[k] for k in range(poles)]
        while len(terms) > 1:
            terms = [a + b for a, b in zip(terms[::2], terms[1::2])] + terms[len(terms) // 2 * 2 :]
        signal_rows[row_at(t), :] = terms[0] + skip_held * row
        return state

    entry = tuple(first_state[pl.ds(k * groups, groups), :] for k in range(poles))
    last = lax.fori_loop(0, rows, with_output, entry, unroll=4)
    for k in range(poles):
        state_out[pl.ds(k * groups, groups), :] = last[k]

    @pl.when(seq == 0)
    def _():
        carry.start()

    @pl.loop(0, groups)
    def _(j):
        lanes = pl.ds(pl.multiple_of(j * 128, 128), 128)

        @pl.loop(0, rows // chunk)
        def _(b):
            r = pl.multiple_of(b * chunk, chunk)
            long = signal_rows[strided(r * groups + j, chunk, groups), :]
            gated_ref[pl.ds(r, chunk), lanes] = (query[pl.ds(r, chunk), lanes] * long).astype(jnp.bfloat16)

    @pl.when(seq == 0)
    def _():
        rim.wait_send()
        carry.wait_send()

    for part in range(PIECES):
        for direction in range(2):

            @pl.loop(0, middle - 1)
            def _(step):
                hop(direction, step, part, step).wait_send()

        hop(part // (PIECES // 2), middle - 1, part, middle - 1).wait_send()


def back_kernel(
    n, gated_ref, tok_ref, w_hbm, out_ref, w_buf, partial, outgoing, incoming, send_sem, recv_sem, w_sem
):
    rows, width = tok_ref.shape
    middle = n // 2
    piece = rows // PIECES
    small = min(32, piece)
    tile = min(256, width)
    me = lax.axis_index("chan")
    pos = ring_position(me, n)
    right = {"chan": ring_index(lax.rem(pos + 1, n), n)}
    left = {"chan": ring_index(lax.rem(pos + n - 1, n), n)}
    ahead = (right, left)

    def w_copy(block):
        away = middle - lax.div(block + 1, 2)
        odd = lax.rem(block, 2)
        target = ring_index(lax.rem(pos + odd * away + (1 - odd) * (n - away), n), n)
        slot = lax.rem(block, W_SLOTS)
        return pltpu.make_async_copy(
            w_hbm.at[:, pl.ds(pl.multiple_of(target * width, 128), width)],
            w_buf.at[slot],
            w_sem.at[slot],
        )

    def hop(direction, step, part):
        span = pl.ds(part * piece, piece)
        return pltpu.make_async_remote_copy(
            src_ref=outgoing.at[direction, step, span, :],
            dst_ref=incoming.at[direction, step, span, :],
            send_sem=send_sem.at[direction, step, part],
            recv_sem=recv_sem.at[direction, step, part],
            device_id=ahead[direction],
            device_id_type=MESH,
        )

    def multiply(block, place):
        slot = lax.rem(block, W_SLOTS)
        w_copy(block).wait()

        @pl.loop(0, width // tile)
        def _(c):
            cols = pl.ds(pl.multiple_of(c * tile, 128), tile)
            partial[place, :, cols] = jnp.dot(
                gated_ref[...], w_buf[slot, :, cols], preferred_element_type=jnp.float32
            )

        @pl.when(block + W_SLOTS < n)
        def _():
            w_copy(block + W_SLOTS).start()

    def send(direction, step, part, place, add):
        @pl.loop(0, piece // small)
        def _(b):
            span = pl.ds(pl.multiple_of(part * piece + b * small, small), small)
            total = partial[place, span, :]
            if add:
                total = total + incoming[direction, step - 1, span, :].astype(jnp.float32)
            outgoing[direction, step, span, :] = total.astype(jnp.bfloat16)

        hop(direction, step, part).start()

    def side(part):
        return part // (PIECES // 2)

    order = [k // 2 + (k % 2) * (PIECES // 2) for k in range(PIECES)]
    for block in range(W_SLOTS):
        w_copy(jnp.int32(block)).start()
    greet((right, left))
    multiply(jnp.int32(0), 0)
    for part in order:
        send(side(part), 0, part, 0, False)
    for direction in range(2):
        multiply(jnp.int32(1 + direction), direction)
    for direction in range(2):
        for part in range(PIECES):
            if side(part) != direction:
                send(direction, 1, part, direction, False)
    for part in order:
        hop(side(part), 0, part).wait_recv()
        send(side(part), 1, part, side(part), True)

    @pl.loop(2, middle)
    def _(step):
        for direction in range(2):
            multiply(2 * step - 1 + direction, direction)
        for k in range(PIECES):
            for direction in range(2):
                part = (k + (1 - direction) * (PIECES // 2)) % PIECES
                hop(direction, step - 1, part).wait_recv()
                send(direction, step, part, direction, True)

    multiply(jnp.int32(n - 1), 0)
    for part in range(PIECES):
        for direction in range(2):
            hop(direction, middle - 1, part).wait_recv()

        @pl.loop(0, piece // small)
        def _(b):
            span = pl.ds(pl.multiple_of(part * piece + b * small, small), small)
            total = partial[0, span, :]
            for direction in range(2):
                total = total + incoming[direction, middle - 1, span, :].astype(jnp.float32)
            out_ref[span, :] = (tok_ref[span, :].astype(jnp.float32) + total).astype(jnp.bfloat16)

    for part in range(PIECES):
        hop(side(part), 0, part).wait_send()
        for direction in range(2):

            @pl.loop(1, middle)
            def _(step):
                hop(direction, step, part).wait_send()


def per_device(n, tokens, norm_gain, in_weight, short_weight, log_decay, residue, skip, out_weight):
    rows, width = tokens.shape
    groups = width // 128
    poles = log_decay.shape[0]
    middle = n // 2
    vmem = pl.BlockSpec(memory_space=pltpu.VMEM)
    anywhere = pl.BlockSpec(memory_space=pl.ANY)
    f32, bf16 = jnp.float32, jnp.bfloat16
    dma = pltpu.SemaphoreType.DMA
    gated = pl.pallas_call(
        functools.partial(front_kernel, n, EPSILON),
        out_shape=jax.ShapeDtypeStruct((rows, width), bf16),
        in_specs=[anywhere, vmem, anywhere, vmem, vmem, vmem, vmem],
        out_specs=vmem,
        scratch_shapes=[
            pltpu.VMEM((n, rows, width), bf16),
            pltpu.VMEM((3, rows + 8, width), f32),
            pltpu.VMEM((W_SLOTS, width, width), bf16),
            pltpu.VMEM((rows, width), bf16),
            pltpu.VMEM((rows, 128), f32),
            pltpu.VMEM((rows, width), f32),
            pltpu.VMEM((rows * groups, 128), f32),
            pltpu.VMEM((poles * groups, 128), f32),
            pltpu.VMEM((poles * groups, 128), f32),
            pltpu.VMEM((groups, 128), f32),
            pltpu.VMEM((3, 8, width), f32),
            pltpu.VMEM((3, 8, width), f32),
            pltpu.VMEM((poles * groups, 128), f32),
            pltpu.VMEM((poles * groups, 128), f32),
            pltpu.VMEM((poles * groups, 128), f32),
            dma((2, middle, PIECES)),
            dma((2, middle, PIECES)),
            dma((W_SLOTS,)),
            dma,
            dma((2,)),
            dma((2,)),
            pltpu.SemaphoreType.REGULAR,
        ],
        compiler_params=pltpu.CompilerParams(
            collective_id=0, has_side_effects=True, vmem_limit_bytes=56 << 20
        ),
    )(tokens, norm_gain[None, :], in_weight, short_weight, log_decay, residue, skip[None, :])
    return pl.pallas_call(
        functools.partial(back_kernel, n),
        out_shape=jax.ShapeDtypeStruct((rows, width), bf16),
        in_specs=[vmem, vmem, anywhere],
        out_specs=vmem,
        scratch_shapes=[
            pltpu.VMEM((W_SLOTS, width, width), bf16),
            pltpu.VMEM((2, rows, width), f32),
            pltpu.VMEM((2, middle, rows, width), bf16),
            pltpu.VMEM((2, middle, rows, width), bf16),
            dma((2, middle, PIECES)),
            dma((2, middle, PIECES)),
            dma((W_SLOTS,)),
        ],
        compiler_params=pltpu.CompilerParams(
            collective_id=1, has_side_effects=True, vmem_limit_bytes=56 << 20
        ),
    )(gated, tokens, out_weight)


def solution(mesh):
    return jax.shard_map(
        functools.partial(per_device, mesh.shape["chan"]),
        mesh=mesh,
        in_specs=(
            P(("groups", "seq"), "chan"),
            P(),
            P(None, None, "chan"),
            P(None, None, "chan"),
            P(None, "chan"),
            P(None, "chan"),
            P("chan"),
            P("chan", None),
        ),
        out_specs=P(("groups", "seq"), "chan"),
        check_vma=False,
    )
```

time: 208 us -> 173 us (0.83)
  Pallas kernels: 204 us -> 170 us
    pallas_call x1, Pallas kernels: 88.2 us -> 49.6 us  [per_device(): pl.pallas_call(functools.partial(back_kernel, n), out_shape=jax.ShapeDtyp...]
    pallas_call x1, Pallas kernels: 116 us -> 121 us  [per_device(): pl.pallas_call(functools.partial(front_kernel, n, EPSILON), out_shape=jax...]
where the time goes in v2:
time: 173 us
  Pallas kernels  170 us (98%)
  local copies, waits for them, and re-layouts  2.26 us (1%)
    pallas_call x1, Pallas kernels, per_device(): pl.pallas_call(functools.partial(front_kernel, n, EPSILON), out_shape=jax...  121 us
    pallas_call x1, Pallas kernels, per_device(): pl.pallas_call(functools.partial(back_kernel, n), out_shape=jax.ShapeDtyp...  49.6 us

profile of v2, /device:TPU:1, one launch (start us, length us, event | category | flops | bytes accessed | tf_op | source)
XLA Modules:
  0.0 172.6 jit_solution(14751008861642713973)
XLA Ops:
  0.0 120.7 %shard_map.82.gated_ref = bf16[512,1024]{1,0:T(8,128)(2,1)} custom-call(bf16[512,1024]{1,0:T(8,128)(2,1)} %tok_ref.1, f32[1,8192]{1,0:T(1,128)} %bitcast.2, bf16[3,8192,1024]{2,1,0:T(8,128)(2,1)} %w_hbm.2, f32[3,7,1024]{2,1,0:T(8,128)} %taps_ref.1, f32[16,1024]{1,0:T(8,128)} %decay_ref.1, f32[16,1024]{1,0:T(8,128)} %res_ref.1, f32[1,1024]{1,0:T(1,128)} %bitcast.3), custom_call_target="tpu_custom_call" | custom-call | tf_op jit(solution)/shard_map/pallas_call | solution.py:433
  120.7 49.6 %shard_map.83 = bf16[512,1024]{1,0:T(8,128)(2,1)} custom-call(bf16[512,1024]{1,0:T(8,128)(2,1)} %shard_map.82.gated_ref, bf16[512,1024]{1,0:T(8,128)(2,1)} %tok_ref.1, bf16[1024,8192]{1,0:T(8,128)(2,1)} %w_hbm.3), custom_call_target="tpu_custom_call" | custom-call | tf_op jit(solution)/shard_map/pallas_call | solution.py:466
  170.4 2.3 %copy.10 = bf16[512,1024]{1,0:T(8,128)(2,1)} copy(bf16[512,1024]{1,0:T(8,128)(2,1)} %shard_map.83) | data formatting | bytes 2097152

commit v3 on v2

--- a/solution.py
+++ b/solution.py
@@ -10,6 +10,7 @@
 EPSILON = 1e-06
 MESH = pl.DeviceIdType.MESH
 PIECES = 4
+OUT_PIECES = 8
 W_SLOTS = 4
 
 
@@ -34,9 +35,22 @@
     return pl.ds(start, size) if stride == 1 else pl.ds(start, size, stride=stride)
 
 
+def out_copy(n, pos, w_hbm, w_buf, w_sem, block):
+    width = w_buf.shape[1]
+    away = n // 2 - lax.div(block + 1, 2)
+    odd = lax.rem(block, 2)
+    target = ring_index(lax.rem(pos + odd * away + (1 - odd) * (n - away), n), n)
+    slot = lax.rem(block, W_SLOTS)
+    return pltpu.make_async_copy(
+        w_hbm.at[:, pl.ds(pl.multiple_of(target * width, 128), width)],
+        w_buf.at[slot],
+        w_sem.at[slot],
+    )
+
+
 def front_kernel(
-    n, eps, tok_hbm, gain_ref, w_hbm, taps_ref, decay_ref, res_ref, skip_ref, gated_ref,
-    held, acc, w_buf, scaled, squares, query, signal_rows, pole, residue, skip_rows,
+    n, eps, tok_hbm, gain_ref, w_hbm, taps_ref, decay_ref, res_ref, skip_ref, out_hbm, out_ref,
+    gated_ref, partial, outgoing, incoming, out_send, out_recv, held, acc, w_buf, scaled, squares, query, signal_rows, pole, residue, skip_rows,
     rim_out, rim_in, state_out, state_in, first_state, send_sem, recv_sem, w_sem, own_sem, pair_send, pair_recv, turn,
 ):
     rows, width = tok_hbm.shape
@@ -192,6 +206,8 @@
     prepare(jnp.int32(n - 1))
     for i in range(3):
         multiply(jnp.int32(n - 1), i)
+    for block in range(W_SLOTS):
+        out_copy(n, pos, out_hbm, w_buf, w_sem, jnp.int32(block)).start()
 
     @pl.loop(0, rows // chunk)
     def _(b):
@@ -292,6 +308,11 @@
             long = signal_rows[strided(r * groups + j, chunk, groups), :]
             gated_ref[pl.ds(r, chunk), lanes] = (query[pl.ds(r, chunk), lanes] * long).astype(jnp.bfloat16)
 
+    back_part(
+        n, gated_ref, held.at[me], out_hbm, out_ref, w_buf, partial, outgoing, incoming,
+        out_send, out_recv, w_sem,
+    )
+
     @pl.when(seq == 0)
     def _():
         rim.wait_send()
@@ -307,12 +328,12 @@
         hop(part // (PIECES // 2), middle - 1, part, middle - 1).wait_send()
 
 
-def back_kernel(
+def back_part(
     n, gated_ref, tok_ref, w_hbm, out_ref, w_buf, partial, outgoing, incoming, send_sem, recv_sem, w_sem
 ):
     rows, width = tok_ref.shape
     middle = n // 2
-    piece = rows // PIECES
+    piece = rows // OUT_PIECES
     small = min(32, piece)
     tile = min(256, width)
     me = lax.axis_index("chan")
@@ -322,15 +343,7 @@
     ahead = (right, left)
 
     def w_copy(block):
-        away = middle - lax.div(block + 1, 2)
-        odd = lax.rem(block, 2)
-        target = ring_index(lax.rem(pos + odd * away + (1 - odd) * (n - away), n), n)
-        slot = lax.rem(block, W_SLOTS)
-        return pltpu.make_async_copy(
-            w_hbm.at[:, pl.ds(pl.multiple_of(target * width, 128), width)],
-            w_buf.at[slot],
-            w_sem.at[slot],
-        )
+        return out_copy(n, pos, w_hbm, w_buf, w_sem, block)
 
     def hop(direction, step, part):
         span = pl.ds(part * piece, piece)
@@ -370,19 +383,16 @@
         hop(direction, step, part).start()
 
     def side(part):
-        return part // (PIECES // 2)
-
-    order = [k // 2 + (k % 2) * (PIECES // 2) for k in range(PIECES)]
-    for block in range(W_SLOTS):
-        w_copy(jnp.int32(block)).start()
-    greet((right, left))
+        return part // (OUT_PIECES // 2)
+
+    order = [k // 2 + (k % 2) * (OUT_PIECES // 2) for k in range(OUT_PIECES)]
     multiply(jnp.int32(0), 0)
     for part in order:
         send(side(part), 0, part, 0, False)
     for direction in range(2):
         multiply(jnp.int32(1 + direction), direction)
     for direction in range(2):
-        for part in range(PIECES):
+        for part in range(OUT_PIECES):
             if side(part) != direction:
                 send(direction, 1, part, direction, False)
     for part in order:
@@ -393,14 +403,14 @@
     def _(step):
         for direction in range(2):
             multiply(2 * step - 1 + direction, direction)
-        for k in range(PIECES):
+        for k in range(OUT_PIECES):
             for direction in range(2):
-                part = (k + (1 - direction) * (PIECES // 2)) % PIECES
+                part = (k + (1 - direction) * (OUT_PIECES // 2)) % OUT_PIECES
                 hop(direction, step - 1, part).wait_recv()
                 send(direction, step, part, direction, True)
 
     multiply(jnp.int32(n - 1), 0)
-    for part in range(PIECES):
+    for part in range(OUT_PIECES):
         for direction in range(2):
             hop(direction, middle - 1, part).wait_recv()
 
@@ -412,7 +422,7 @@
                 total = total + incoming[direction, middle - 1, span, :].astype(jnp.float32)
             out_ref[span, :] = (tok_ref[span, :].astype(jnp.float32) + total).astype(jnp.bfloat16)
 
-    for part in range(PIECES):
+    for part in range(OUT_PIECES):
         hop(side(part), 0, part).wait_send()
         for direction in range(2):
 
@@ -430,12 +440,18 @@
     anywhere = pl.BlockSpec(memory_space=pl.ANY)
     f32, bf16 = jnp.float32, jnp.bfloat16
     dma = pltpu.SemaphoreType.DMA
-    gated = pl.pallas_call(
+    return pl.pallas_call(
         functools.partial(front_kernel, n, EPSILON),
         out_shape=jax.ShapeDtypeStruct((rows, width), bf16),
-        in_specs=[anywhere, vmem, anywhere, vmem, vmem, vmem, vmem],
+        in_specs=[anywhere, vmem, anywhere, vmem, vmem, vmem, vmem, anywhere],
         out_specs=vmem,
         scratch_shapes=[
+            pltpu.VMEM((rows, width), bf16),
+            pltpu.VMEM((2, rows, width), f32),
+            pltpu.VMEM((2, middle, rows, width), bf16),
+            pltpu.VMEM((2, middle, rows, width), bf16),
+            dma((2, middle, OUT_PIECES)),
+            dma((2, middle, OUT_PIECES)),
             pltpu.VMEM((n, rows, width), bf16),
             pltpu.VMEM((3, rows + 8, width), f32),
             pltpu.VMEM((W_SLOTS, width, width), bf16),
@@ -462,25 +478,7 @@
         compiler_params=pltpu.CompilerParams(
             collective_id=0, has_side_effects=True, vmem_limit_bytes=56 << 20
         ),
-    )(tokens, norm_gain[None, :], in_weight, short_weight, log_decay, residue, skip[None, :])
-    return pl.pallas_call(
-        functools.partial(back_kernel, n),
-        out_shape=jax.ShapeDtypeStruct((rows, width), bf16),
-        in_specs=[vmem, vmem, anywhere],
-        out_specs=vmem,
-        scratch_shapes=[
-            pltpu.VMEM((W_SLOTS, width, width), bf16),
-            pltpu.VMEM((2, rows, width), f32),
-            pltpu.VMEM((2, middle, rows, width), bf16),
-            pltpu.VMEM((2, middle, rows, width), bf16),
-            dma((2, middle, PIECES)),
-            dma((2, middle, PIECES)),
-            dma((W_SLOTS,)),
-        ],
-        compiler_params=pltpu.CompilerParams(
-            collective_id=1, has_side_effects=True, vmem_limit_bytes=56 << 20
-        ),
-    )(gated, tokens, out_weight)
+    )(tokens, norm_gain[None, :], in_weight, short_weight, log_decay, residue, skip[None, :], out_weight)
 
 
 def solution(mesh):

time: 173 us -> 174 us (level)
    pallas_call x1, Pallas kernels: 121 us -> 171 us  [per_device(): pl.pallas_call(functools.partial(front_kernel, n, EPSILON), out_shape=jax...]
    pallas_call x1 -> x0, Pallas kernels: 49.6 us -> none  [per_device(): pl.pallas_call(functools.partial(back_kernel, n), out_shape=jax.ShapeDtyp...]
where the time goes in v3:
time: 174 us; the launch traced here: 173 us
  Pallas kernels  171 us (98%)
  local copies, waits for them, and re-layouts  2.26 us (1%)
    pallas_call x1, Pallas kernels, per_device(): pl.pallas_call(functools.partial(front_kernel, n, EPSILON), out_shape=jax...  171 us

profile of v3, /device:TPU:1, one launch (start us, length us, event | category | flops | bytes accessed | tf_op | source)
XLA Modules:
  0.0 173.5 jit_solution(49558483103610150)
XLA Ops:
  0.0 171.2 %shard_map.82 = bf16[512,1024]{1,0:T(8,128)(2,1)} custom-call(bf16[512,1024]{1,0:T(8,128)(2,1)} %tok_hbm.1, f32[1,8192]{1,0:T(1,128)} %bitcast.2, bf16[3,8192,1024]{2,1,0:T(8,128)(2,1)} %w_hbm.1, f32[3,7,1024]{2,1,0:T(8,128)} %taps_ref.1, f32[16,1024]{1,0:T(8,128)} %decay_ref.1, f32[16,1024]{1,0:T(8,128)} %res_ref.1, f32[1,1024]{1,0:T(1,128)} %bitcast.3, ...), custom_call_target="tpu_custom_call" | custom-call | tf_op jit(solution)/shard_map/pallas_call | solution.py:443
  171.2 2.3 %copy.10 = bf16[512,1024]{1,0:T(8,128)(2,1)} copy(bf16[512,1024]{1,0:T(8,128)(2,1)} %shard_map.82) | data formatting | bytes 2097152
